TPU v7x, 128 devices: a whole 4x4x4 slice. The times are simulated.
128 devices in a mesh: animal: 16 (over y_lo, x, core), marker: 8 (over z, y_hi).
Axes of the slice: x: 4, y: 4 (y_hi: 2, y_lo: 2; y = y_hi * 2 + y_lo), z: 4, core: 2. Of those that a mesh axis runs over, the one named last changes fastest.
Arguments:
- genotypes: bfloat16 [49152, 25600], P('animal', 'marker'), may hold values from -4 to 4
- direction: bfloat16 [25600, 256], P('marker'), may hold values from -6 to 6
- ridge: float32 [25600], P('marker'), may hold values from 0.5 to 2
- send_list: int32 [16, 16, 2], P('animal'), may hold values from 0 to 23, as said below
- rel_index: int32 [384, 4], P('animal'), may hold values from 0 to 55, as said below
- rel_count: int32 [384], P('animal'), may hold values from 1 to 4, as said below
- rel_prec: bfloat16 [384, 4, 128, 128], P('animal'), may hold values from -0.375 to 0.375
Outputs:
- gradient: float32 [25600, 256], P(('marker', 'animal'))
Inputs may be any that keep to these rules, and one draw needn't show every extreme that they name: `send_list`: every entry names one of the sender's own 24 blocks. `rel_index`: entry j of block g indexes g's device's source table; entry 0 is g's own block, g % 24. `rel_count`: the first block of every device has 4 live slots.
All inputs are finite; a program needn't handle non-finite values.
Results may differ from a plain program's by a relative error of at most 0.0033.
Values may be sent and summed in bfloat16 or wider, within the bound.
A program may use at most 128 MiB of HBM per device.

v0:
```python
import math

import jax
import jax.numpy as jnp
from jax import lax
from jax.sharding import PartitionSpec as P

MARKERS = 25600
BLK = 128


def pedigree(animal_rows, send_list, rel_index, rel_count, rel_prec):
    block_total = animal_rows.shape[0] // BLK
    col_total = animal_rows.shape[1]
    blocked = animal_rows.reshape(block_total, BLK, col_total)
    outgoing = blocked[send_list[0]]
    incoming = lax.all_to_all(outgoing, "animal", split_axis=0, concat_axis=0, tiled=True)
    source_table = jnp.concatenate([blocked, incoming.reshape(-1, BLK, col_total)], axis=0)
    active = jnp.arange(rel_index.shape[1], dtype=jnp.int32)[None, :] < rel_count[:, None]
    gathered = source_table[rel_index]
    gathered = jnp.where(active[:, :, None, None], gathered, jnp.zeros_like(gathered))
    accumulated = jnp.einsum(
        "bjrc,bjck->brk", rel_prec, gathered, preferred_element_type=jnp.float32
    )
    return accumulated.astype(jnp.bfloat16).reshape(block_total * BLK, col_total)


def local(genotypes, direction, ridge, send_list, rel_index, rel_count, rel_prec):
    anim_rows = genotypes.shape[0]
    mark_rows = genotypes.shape[1]
    group_count = lax.axis_size("animal")
    input_scale = 1.0 / math.sqrt(MARKERS)
    partial_value = jnp.dot(genotypes, direction, preferred_element_type=jnp.float32)
    summed = lax.psum(partial_value, "marker")
    shared = (summed * input_scale).astype(jnp.bfloat16)
    effects = pedigree(shared, send_list, rel_index, rel_count, rel_prec)
    row_count = mark_rows // group_count
    gradient = lax.psum_scatter(
        lax.dot_general(
            genotypes, effects, (((0,), (0,)), ((), ())), preferred_element_type=jnp.float32
        ),
        "animal",
        scatter_dimension=0,
        tiled=True,
    )
    output_scale = 1.0 / math.sqrt(group_count * anim_rows)
    row_start = lax.axis_index("animal") * row_count
    own_ridge = lax.dynamic_slice_in_dim(ridge, row_start, row_count, 0)
    own_direction = lax.dynamic_slice_in_dim(direction, row_start, row_count, 0)
    return gradient * output_scale + own_ridge[:, None] * own_direction.astype(jnp.float32)


def solution(mesh):
    in_specs = (
        P("animal", "marker"),
        P("marker", None),
        P("marker"),
        P("animal", None, None),
        P("animal", None),
        P("animal"),
        P("animal", None, None, None),
    )
    out_specs = P(("marker", "animal"), None)
    return jax.shard_map(local, mesh=mesh, in_specs=in_specs, out_specs=out_specs, check_vma=False)
```

profile of v0, /device:TPU:0, one launch (start us, length us, event | category | flops | bytes accessed | tf_op | source)
XLA Modules:
  0.0 313.6 jit_solution(2736367599061070553)
XLA Ops:
  6.5 0.0 copy-start
  6.5 0.0 all-reduce.2.cloned.1.call-start
  6.5 11.2 %fusion.7 = f32[3072,256]{1,0:T(8,128)} fusion(bf16[3072,3200]{1,0:T(8,128)(2,1)} %param.7, bf16[3200,256]{1,0:T(8,128)(2,1)} %param.8), kind=kOutput, calls=%fused_computation.18 | convolution fusion | flops 5033164800 | bytes 24444928 | tf_op jit(solution)/shard_map/dot_general | solution.py:33
  17.7 0.0 copy-start.2
  17.7 0.0 all-reduce.2.cloned.1.call-update
  17.8 0.7 copy-done.2
  18.4 0.1 copy.16
  18.5 0.1 reshape.64
  18.6 147.9 %all-reduce.2.cloned.1.call-done = f32[3072,256]{1,0:T(8,128)} async-done(((f32[3072,256]{1,0:T(8,128)}), f32[3072,256]{1,0:T(8,128)}) %all-reduce.2.cloned.1.call-update) | async-done | bytes 3145744 | tf_op jit(solution)/shard_map/psum | solution.py:34
  166.5 3.4 %multiply_convert_fusion = bf16[3072,256]{1,0:T(8,128)(2,1)} fusion(f32[3072,256]{1,0:T(8,128)} %all-reduce.2.cloned.1.call-done), kind=kLoop, calls=%fused_computation.9 | loop fusion | flops 1572864 | bytes 4718592 | tf_op jit(solution)/shard_map/convert_element_type | solution.py:35
  169.9 3.4 %gather_fusion = bf16[32,128,256]{2,1,0:T(8,128)(2,1)} fusion(bf16[24,128,256]{2,1,0:T(8,128)(2,1)} %bitcast.22, s32[1024]{0:T(1024)S(1)} %pad_clamp_fusion.1), kind=kCustom, calls=%fused_computation | custom fusion | bytes 4194432 | tf_op jit(solution)/shard_map/gather | solution.py:16
  173.3 0.0 copy-start.1
  173.3 0.0 copy-start.3
  173.3 4.6 %all-to-all-start = ((bf16[16,2,128,256]{3,2,1,0:T(8,128)(2,1)}), bf16[16,2,128,256]{3,2,1,0:T(8,128)(2,1)}, u32[]{:S(2)}, u32[]{:S(2)}) async-start(bf16[16,2,128,256]{3,2,1,0:T(8,128)(2,1)} %bitcast.24), calls=%async_computation | async-start | bytes 4194304 | tf_op jit(solution)/shard_map/all_to_all | solution.py:17
  177.9 0.0 reduce-scatter.4.cloned.1.call-start
  178.0 0.0 copy-done.1
  178.0 0.1 copy.17
  178.1 0.1 reshape.72
  178.2 0.0 copy-done.3
  178.2 0.1 iota_compare_fusion
  178.3 27.7 %all-to-all-done = bf16[16,2,128,256]{3,2,1,0:T(8,128)(2,1)} async-done(((bf16[16,2,128,256]{3,2,1,0:T(8,128)(2,1)}), bf16[16,2,128,256]{3,2,1,0:T(8,128)(2,1)}, u32[]{:S(2)}, u32[]{:S(2)}) %all-to-all-start) | async-done | bytes 2097184 | tf_op jit(solution)/shard_map/all_to_all | solution.py:17
  206.0 4.2 %pad_maximum_fusion = bf16[56,128,256]{2,1,0:T(8,128)(2,1)} fusion(bf16[32,128,256]{2,1,0:T(8,128)(2,1)} %bitcast.3, bf16[24,128,256]{2,1,0:T(8,128)(2,1)} %bitcast.23), kind=kLoop, calls=%fused_computation.6 | loop fusion | flops 1835008 | bytes 7340032 | tf_op jit(solution)/shard_map/concatenate | solution.py:18
  210.2 8.1 %gather_fusion.1 = bf16[96,128,256]{2,1,0:T(8,128)(2,1)} fusion(bf16[56,128,256]{2,1,0:T(8,128)(2,1)} %pad_maximum_fusion, s32[1024]{0:T(1024)S(1)} %pad_clamp_fusion), kind=kCustom, calls=%fused_computation.1 | custom fusion | bytes 12583296 | tf_op jit(solution)/shard_map/gather | solution.py:20
  218.2 0.0 copy-done
  218.2 4.1 %bitcast_convert_fusion = bf16[24,256,128]{1,2,0:T(8,128)(2,1)S(1)} fusion(bf16[24,4,128,128]{3,2,1,0:T(8,128)(2,1)S(1)} %copy-done, bf16[24,4,128,256]{3,2,1,0:T(8,128)(2,1)} %bitcast.25, pred[24,4]{1,0:T(8,128)(4,1)S(1)} %iota_compare_fusion), kind=kOutput, calls=%fused_computation.7 | convolution fusion | flops 809238528 | bytes 11010144 | tf_op jit(solution)/shard_map/bjrc,bjck->brk/dot_general | solution.py:22
  222.3 11.2 %convolution_bitcast_fusion = f32[3200,256]{0,1:T(8,128)} fusion(bf16[3072,256]{1,0:T(8,128)(2,1)S(1)} %bitcast.26, bf16[3072,3200]{1,0:T(8,128)(2,1)} %param.7), kind=kOutput, calls=%fused_computation.5 | convolution fusion | flops 5033164800 | bytes 24510464 | tf_op jit(solution)/shard_map/dot_general | solution.py:39
  233.6 4.8 %copy.21 = f32[3200,256]{1,0:T(8,128)} copy(f32[3200,256]{0,1:T(8,128)} %convolution_bitcast_fusion) | data formatting | bytes 6553600
  238.4 0.0 reduce-scatter.4.cloned.1.call-update
  238.4 0.9 constant_dynamic-slice_fusion
  239.3 0.1 copy.23
  239.4 0.8 dynamic_slice.6
  240.2 63.0 %reduce-scatter.4.cloned.1.call-done = f32[200,256]{1,0:T(8,128)} async-done(((f32[3200,256]{1,0:T(8,128)}), f32[200,256]{1,0:T(8,128)}) %reduce-scatter.4.cloned.1.call-update) | async-done | bytes 204816
  303.2 1.1 copy.22
  304.3 0.7 multiply_add_fusion
  305.0 1.7 copy.19
  (4 shorter events, 0.0 us)
Async XLA Ops:
  6.5 211.7 %copy-start = (bf16[24,4,128,128]{3,2,1,0:T(8,128)(2,1)S(1)}, bf16[24,4,128,128]{3,2,1,0:T(8,128)(2,1)}, u32[]{:S(2)}) copy-start(bf16[24,4,128,128]{3,2,1,0:T(8,128)(2,1)} %param.13) | copy-start | bytes 9437188
  6.5 160.0 %all-reduce.2.cloned.1.call-start = ((), (), s32[]{:S(2)}) async-start(), calls=%async_computation.2 | async-start | bytes 6291456 | tf_op jit(solution)/shard_map/psum | solution.py:34
  17.7 0.7 copy-start.2
  173.3 4.6 %copy-start.1 = (s32[24,4]{0,1:T(4,128)S(1)}, s32[24,4]{0,1:T(4,128)}, u32[]{:S(2)}) copy-start(s32[24,4]{0,1:T(4,128)} %param.11) | copy-start | bytes 1156
  173.3 4.9 %copy-start.3 = (s32[24]{0:T(128)S(1)}, s32[24]{0:T(128)}, u32[]{:S(2)}) copy-start(s32[24]{0:T(128)} %param.12) | copy-start | bytes 292
  173.3 32.6 %all-to-all-start = ((bf16[16,2,128,256]{3,2,1,0:T(8,128)(2,1)}), bf16[16,2,128,256]{3,2,1,0:T(8,128)(2,1)}, u32[]{:S(2)}, u32[]{:S(2)}) async-start(bf16[16,2,128,256]{3,2,1,0:T(8,128)(2,1)} %bitcast.24), calls=%async_computation | async-start | bytes 4194304 | tf_op jit(solution)/shard_map/all_to_all | solution.py:17
  177.9 125.3 %reduce-scatter.4.cloned.1.call-start = ((), (), s32[]{:S(2)}) async-start(), calls=%async_computation.3 | async-start | bytes 3481600
Sparse Core Ops, SparseCore 0:
  17.9 148.6 all-reduce.1
  238.5 64.6 reduce-scatter.3
where the time goes:
time: 314 us
  waiting for transfers between devices  239 us (76%)
  matrix products  26.5 us (8%)
  local copies, waits for them, and re-layouts  21.9 us (7%)
  between operations  13.5 us (4%)
  other arithmetic  8.45 us (3%)
  starting transfers between devices  4.62 us (1%)
    psum x1, waiting for transfers between devices, local(): summed = lax.psum(partial_value, 'marker')  148 us
    unnamed x3, waiting for transfers between devices  63 us
    all_to_all x1, waiting for transfers between devices, pedigree(): lax.all_to_all(outgoing, 'animal', split_axis=0, concat_axis=0, tiled=True)  27.7 us
    dot_general x1, matrix products, local(): lax.dot_general(genotypes, effects, (((0,), (0,)), ((), ())), preferred_e...  11.2 us
    dot_general x1, matrix products, local(): jnp.dot(genotypes, direction, preferred_element_type=jnp.float32)  11.2 us
    gather x1, local copies, waits for them, and re-layouts, pedigree(): gathered = source_table[rel_index]  8.05 us
    unnamed x11, local copies, waits for them, and re-layouts  6.64 us
  transfers between devices with their start and end apart: 3, of which 3 were waited for; matrix products, arithmetic and copies ran while one was open for 1% of the time, Pallas kernels for 0%

commit v1 on v0

v1 whole, which is shorter than its diff:
```python
import math

import jax
import jax.numpy as jnp
from jax import lax
from jax.experimental import pallas as pl
from jax.experimental.pallas import tpu as pltpu
from jax.sharding import PartitionSpec as P

MESH = pl.DeviceIdType.MESH
MARKERS = 25600
ANIMALS = 49152
BLK = 128
K = 256
NB = 24
NREL = 4
PEERS = 16
SLOTS = 2
ROWS = NB * BLK
COLS = 3200
OWN = 200
KO = 32
CB = 4
W = CB * BLK
NC = NB // CB
F32 = jnp.float32
BF16 = jnp.bfloat16


def kernel(
    geno, direc, prec, send_list, rel_index, rel_count, out,
    g_v, d_v, prec_v, st, r1p, r1m, r2p, r2m, ry, t_loc, table, stage, rt, ot, o_full, cx,
    d1, d2p, d2m, dy, e1p, e1m, e2p, e2m, ey,
    ld_sem, ldg_sem, a_send, a_recv, b_send, b_recv, c_send, c_recv, x_send, x_recv, d_send, d_recv,
):
    a = lax.axis_index("animal")
    m = lax.axis_index("marker")
    z, yh = m // 2, m % 2
    zp, zm, zo = (z + 1) % 4, (z + 3) % 4, (z + 2) % 4
    up, down, across = zp * 2 + yh, zm * 2 + yh, z * 2 + 1 - yh
    yl, x, core = a // 8, (a // 2) % 4, a % 2
    xp, xm, xo = (x + 1) % 4, (x + 3) % 4, (x + 2) % 4
    right, left = yl * 8 + xp * 2 + core, yl * 8 + xm * 2 + core
    beside, sibling = (1 - yl) * 8 + x * 2 + core, yl * 8 + x * 2 + 1 - core

    def load_g(c):
        rows = pl.ds(pl.multiple_of(c * W, W), W)
        return pltpu.make_async_copy(geno.at[rows], g_v.at[rows], ldg_sem.at[c])

    load_d = pltpu.make_async_copy(direc, d_v, ld_sem.at[0])
    load_p = pltpu.make_async_copy(prec, prec_v, ld_sem.at[1])

    def remote(src, dst, send, recv, **device):
        return pltpu.make_async_remote_copy(
            src_ref=src, dst_ref=dst, send_sem=send, recv_sem=recv, device_id=device, device_id_type=MESH
        )

    load_d.start()
    load_g(0).start()
    load_g(1).start()
    barrier = pltpu.get_barrier_semaphore()

    def greet(i, carry):
        pl.semaphore_signal(barrier, inc=1, device_id={"animal": (a + i) % PEERS}, device_id_type=MESH)
        return carry

    lax.fori_loop(1, PEERS, greet, 0)
    for other in (up, down, across):
        pl.semaphore_signal(barrier, inc=1, device_id={"marker": other}, device_id_type=MESH)
    load_d.wait()

    def krows(start, size):
        return pl.ds(pl.multiple_of(start, KO), size)

    def a1p(c):
        return remote(st.at[c, krows(zo * 64, KO)], r1p.at[c], a_send.at[0, c], a_recv.at[0, c], marker=up)

    def a1m(c):
        return remote(st.at[c, krows(zo * 64 + KO, KO)], r1m.at[c], a_send.at[1, c], a_recv.at[1, c], marker=down)

    def a2p(c):
        return remote(st.at[c, krows(zp * 64, 64)], r2p.at[c], a_send.at[2, c], a_recv.at[2, c], marker=up)

    def a2m(c):
        return remote(st.at[c, krows(zm * 64, 64)], r2m.at[c], a_send.at[3, c], a_recv.at[3, c], marker=down)

    def ay(c):
        return remote(
            st.at[c, krows(z * 64 + (1 - yh) * KO, KO)], ry.at[c], a_send.at[4, c], a_recv.at[4, c], marker=across
        )

    def step_a(it, carry):
        @pl.when(it < NC)
        def _():
            c = it

            @pl.when(c + 2 < NC)
            def _():
                load_g(c + 2).start()

            @pl.when(c == NC - 1)
            def _():
                load_p.start()

            load_g(c).wait()
            for half in range(2):
                rows = pl.ds(pl.multiple_of(c * W + half * 256, 256), 256)
                part = jnp.dot(g_v[rows, :], d_v[...], preferred_element_type=F32)
                st[c, :, half * 256 : half * 256 + 256] = part.T

            @pl.when(c == 0)
            def _():
                pl.semaphore_wait(barrier, PEERS - 1 + 3)

            a1p(c).start()
            a1m(c).start()

        @pl.when((it >= 1) & (it < NC + 1))
        def _():
            c = it - 1
            a1p(c).wait_recv()
            own = krows(zp * 64, KO)
            st[c, own] = st[c, own] + r1p[c]
            a2p(c).start()
            a1m(c).wait_recv()
            low = krows(zm * 64 + KO, KO)
            st[c, low] = st[c, low] + r1m[c]
            a2m(c).start()

        @pl.when((it >= 2) & (it < NC + 2))
        def _():
            c = it - 2
            a2p(c).wait_recv()
            a2m(c).wait_recv()
            own = krows(z * 64, 64)
            st[c, own] = st[c, own] + (r2p[c] + r2m[c])
            ay(c).start()

        @pl.when(it >= 3)
        def _():
            c = it - 3
            ay(c).wait_recv()
            done = st[c, krows(z * 64 + yh * KO, KO)] + ry[c]
            done = (done * (1.0 / math.sqrt(MARKERS))).astype(BF16)
            for b in range(CB):
                t_loc[c * CB + b] = done[:, b * BLK : (b + 1) * BLK]
                table[c * CB + b] = done[:, b * BLK : (b + 1) * BLK]

        return carry

    lax.fori_loop(0, NC + 3, step_a, 0)

    def b_copy(e, p):
        return remote(
            stage.at[e], table.at[pl.ds(NB + SLOTS * p, SLOTS)], b_send.at[e], b_recv.at[p], animal=e
        )

    def step_b(i, carry):
        e = (a + i) % PEERS
        for s in range(SLOTS):
            stage[e, s] = t_loc[send_list[0, e, s]]
        b_copy(e, a).start()
        return carry

    lax.fori_loop(1, PEERS, step_b, 0)
    for s in range(SLOTS):
        table[NB + SLOTS * a + s] = t_loc[send_list[0, a, s]]
    load_p.wait()

    def wait_b(i, carry):
        p = (a + i) % PEERS
        b_copy(p, p).wait_recv()
        return carry

    lax.fori_loop(1, PEERS, wait_b, 0)

    def c_copy(kind, c, owner, to):
        rows = krows(owner * KO, KO)
        return remote(rt.at[c, rows], rt.at[c, rows], c_send.at[kind, c], c_recv.at[kind, c], marker=to)

    def gather_in(kind, c):
        owner = (across, zm * 2 + yh, zp * 2 + yh, zm * 2 + 1 - yh, zp * 2 + 1 - yh, zo * 2 + yh, zo * 2 + 1 - yh)[kind]
        return c_copy(kind, c, owner, up)

    ot[...] = jnp.zeros_like(ot)

    def step_c(it, carry):
        @pl.when(it < NC)
        def _():
            c = it
            for b in range(CB):
                g = c * CB + b
                count = rel_count[g]
                picked = []
                for j in range(NREL):
                    block = table[rel_index[g, j]]
                    picked.append(jnp.where(j < count, block, jnp.zeros_like(block)))
                total = lax.dot_general(
                    jnp.concatenate(picked, axis=1),
                    jnp.concatenate([prec_v[g, j] for j in range(NREL)], axis=1),
                    (((1,), (1,)), ((), ())),
                    preferred_element_type=F32,
                )
                rt[c, krows(m * KO, KO), b * BLK : (b + 1) * BLK] = total.astype(BF16)
            c_copy(1, c, m, up).start()
            c_copy(2, c, m, down).start()
            c_copy(0, c, m, across).start()

        @pl.when((it >= 1) & (it < NC + 1))
        def _():
            c = it - 1
            gather_in(0, c).wait_recv()
            c_copy(3, c, across, up).start()
            c_copy(4, c, across, down).start()

        @pl.when((it >= 2) & (it < NC + 2))
        def _():
            c = it - 2
            gather_in(1, c).wait_recv()
            c_copy(5, c, zm * 2 + yh, up).start()
            gather_in(4, c).wait_recv()
            c_copy(6, c, zp * 2 + 1 - yh, down).start()

        @pl.when(it >= 3)
        def _():
            c = it - 3
            for kind in (2, 3, 5, 6):
                gather_in(kind, c).wait_recv()
            rows = pl.ds(pl.multiple_of(c * W, W), W)
            lhs = rt[c]

            def tile(n, inner):
                cols = pl.ds(pl.multiple_of(n * 256, 256), 256)
                ot[:, cols] += jnp.dot(lhs, g_v[rows, cols], preferred_element_type=F32)
                return inner

            lax.fori_loop(0, COLS // 256, tile, 0)
            ot[:, COLS - 128 :] += jnp.dot(lhs, g_v[rows, COLS - 128 :], preferred_element_type=F32)

        return carry

    lax.fori_loop(0, NC + 3, step_c, 0)

    def turn(n, carry):
        cols = pl.ds(pl.multiple_of(n * 128, 128), 128)
        o_full[cols, :] = ot[:, cols].T
        return carry

    lax.fori_loop(0, COLS // 128, turn, 0)

    def owner_rows(q, side):
        return pl.ds(pl.multiple_of((2 * q + side) * OWN, 8), OWN)

    def x_copy(q):
        return remote(o_full.at[owner_rows(q, 1 - core)], cx.at[q], x_send.at[q], x_recv.at[q], animal=sibling)

    order = (xo, 4 + xo, 4 + xp, xm, xp, 4 + xm, x, 4 + x)
    for q in order:
        x_copy(q).start()

    def chip_sum(q):
        x_copy(q).wait_recv()
        return o_full[owner_rows(q, core), :] + cx[q]

    def d_copy(kind):
        src, dst, to = (
            (d1.at[0], e1p, right), (d1.at[1], e1m, left),
            (d2p.at[0], e2p.at[0], right), (d2p.at[1], e2p.at[1], right),
            (d2m.at[0], e2m.at[0], left), (d2m.at[1], e2m.at[1], left),
            (dy, ey, beside),
        )[kind]
        return remote(src, dst, d_send.at[kind], d_recv.at[kind], animal=to)

    d1[0] = chip_sum(xo).astype(BF16)
    d_copy(0).start()
    d1[1] = chip_sum(4 + xo).astype(BF16)
    d_copy(1).start()
    d2p[1] = chip_sum(4 + xp).astype(BF16)
    d_copy(3).start()
    d2m[0] = chip_sum(xm).astype(BF16)
    d_copy(4).start()
    near = chip_sum(xp)
    d_copy(0).wait_recv()
    d2p[0] = (near + e1p[...].astype(F32)).astype(BF16)
    d_copy(2).start()
    near = chip_sum(4 + xm)
    d_copy(1).wait_recv()
    d2m[1] = (near + e1m[...].astype(F32)).astype(BF16)
    d_copy(5).start()
    x_copy(x).wait_recv()
    x_copy(4 + x).wait_recv()
    for kind in (2, 3, 4, 5):
        d_copy(kind).wait_recv()

    def ring_sum(side):
        q = side * 4 + x
        own = o_full[owner_rows(q, core), :] + cx[q]
        return own + e2p[side].astype(F32) + e2m[side].astype(F32)

    dy[...] = ring_sum(1 - yl).astype(BF16)
    d_copy(6).start()
    mine = ring_sum(yl)
    d_copy(6).wait_recv()
    out[...] = mine + ey[...].astype(F32)

    def drain(c, carry):
        for copy in (a1p, a1m, a2p, a2m, ay):
            copy(c).wait_send()
        for kind in range(7):
            c_copy(kind, c, m, up).wait_send()
        return carry

    lax.fori_loop(0, NC, drain, 0)

    def drain_b(i, carry):
        b_copy((a + i) % PEERS, a).wait_send()
        return carry

    lax.fori_loop(1, PEERS, drain_b, 0)
    for q in range(8):
        x_copy(q).wait_send()
    for kind in range(7):
        d_copy(kind).wait_send()


def local(genotypes, direction, ridge, send_list, rel_index, rel_count, rel_prec):
    hbm = pl.BlockSpec(memory_space=pl.ANY)
    smem = pl.BlockSpec(memory_space=pltpu.SMEM)
    vmem = pl.BlockSpec(memory_space=pltpu.VMEM)
    dma = pltpu.SemaphoreType.DMA
    gradient = pl.pallas_call(
        kernel,
        out_shape=jax.ShapeDtypeStruct((OWN, K), F32),
        in_specs=[hbm, hbm, hbm, smem, smem, smem],
        out_specs=vmem,
        scratch_shapes=[
            pltpu.VMEM((ROWS, COLS), BF16),
            pltpu.VMEM((COLS, K), BF16),
            pltpu.VMEM((NB, NREL, BLK, BLK), BF16),
            pltpu.VMEM((NC, K, W), F32),
            pltpu.VMEM((NC, KO, W), F32),
            pltpu.VMEM((NC, KO, W), F32),
            pltpu.VMEM((NC, 64, W), F32),
            pltpu.VMEM((NC, 64, W), F32),
            pltpu.VMEM((NC, KO, W), F32),
            pltpu.VMEM((NB, KO, BLK), BF16),
            pltpu.VMEM((NB + PEERS * SLOTS, KO, BLK), BF16),
            pltpu.VMEM((PEERS, SLOTS, KO, BLK), BF16),
            pltpu.VMEM((NC, K, W), BF16),
            pltpu.VMEM((K, COLS), F32),
            pltpu.VMEM((COLS, K), F32),
            pltpu.VMEM((8, OWN, K), F32),
            pltpu.VMEM((2, OWN, K), BF16),
            pltpu.VMEM((2, OWN, K), BF16),
            pltpu.VMEM((2, OWN, K), BF16),
            pltpu.VMEM((OWN, K), BF16),
            pltpu.VMEM((OWN, K), BF16),
            pltpu.VMEM((OWN, K), BF16),
            pltpu.VMEM((2, OWN, K), BF16),
            pltpu.VMEM((2, OWN, K), BF16),
            pltpu.VMEM((OWN, K), BF16),
            dma((2,)), dma((NC,)),
            dma((5, NC)), dma((5, NC)),
            dma((PEERS,)), dma((PEERS,)),
            dma((7, NC)), dma((7, NC)),
            dma((8,)), dma((8,)),
            dma((7,)), dma((7,)),
        ],
        compiler_params=pltpu.CompilerParams(
            collective_id=0, has_side_effects=True, vmem_limit_bytes=63000000
        ),
    )(genotypes, direction, rel_prec, send_list, rel_index, rel_count)
    row_start = lax.axis_index("animal") * OWN
    own_ridge = lax.dynamic_slice_in_dim(ridge, row_start, OWN, 0)
    own_direction = lax.dynamic_slice_in_dim(direction, row_start, OWN, 0)
    return gradient * (1.0 / math.sqrt(ANIMALS)) + own_ridge[:, None] * own_direction.astype(F32)


def solution(mesh):
    in_specs = (
        P("animal", "marker"),
        P("marker", None),
        P("marker"),
        P("animal", None, None),
        P("animal", None),
        P("animal"),
        P("animal", None, None, None),
    )
    out_specs = P(("marker", "animal"), None)
    return jax.shard_map(local, mesh=mesh, in_specs=in_specs, out_specs=out_specs, check_vma=False)
```

time: 314 us -> 104 us (0.33)
  waiting for transfers between devices: 239 us -> 0 us
  Pallas kernels: 0 us -> 98 us
  matrix products: 26.5 us -> 0 us
  local copies, waits for them, and re-layouts: 21.9 us -> 3.48 us
  between operations: 13.5 us -> 0.02 us
  other arithmetic: 8.45 us -> 1.77 us
  starting transfers between devices: 4.62 us -> 0 us
    psum x1 -> x0, waiting for transfers between devices: 148 us -> none  [local(): summed = lax.psum(partial_value, 'marker')]
    pallas_call x0 -> x1, Pallas kernels: none -> 98 us  [local(): pl.pallas_call(kernel, out_shape=jax.ShapeDtypeStruct((OWN, K), F32), in_...]
    unnamed x3 -> x0, waiting for transfers between devices: 63 us -> none
    all_to_all x1 -> x0, waiting for transfers between devices: 27.7 us -> none  [pedigree(): lax.all_to_all(outgoing, 'animal', split_axis=0, concat_axis=0, tiled=True)]
    dot_general x3 -> x0, matrix products: 26.5 us -> none  [the longest x1 11.2 us: local(): lax.dot_general(genotypes, effects, (((0,), (0,)), ((), ())), preferred_e...]
    gather x2 -> x0, local copies, waits for them, and re-layouts: 11.4 us -> none  [the longest x1 8.05 us: pedigree(): gathered = source_table[rel_index]]
    all_to_all x1 -> x0, starting transfers between devices: 4.58 us -> none  [pedigree(): lax.all_to_all(outgoing, 'animal', split_axis=0, concat_axis=0, tiled=True)]
    concatenate x1 -> x0, other arithmetic: 4.22 us -> none  [pedigree(): jnp.concatenate([blocked, incoming.reshape(-1, BLK, col_total)], axis=0)]
  transfers between devices with their start and end apart: 3 -> 0, of which waited for: 3 -> 0; matrix products, arithmetic and copies ran while one was open for 1% -> 0% of each run, Pallas kernels for 0% -> 0%
where the time goes in v1:
time: 104 us; the launch traced here: 103 us
  Pallas kernels  98 us (94%)
  local copies, waits for them, and re-layouts  3.48 us (3%)
  other arithmetic  1.77 us (2%)
    pallas_call x1, Pallas kernels, local(): pl.pallas_call(kernel, out_shape=jax.ShapeDtypeStruct((OWN, K), F32), in_...  98 us
    unnamed x2, local copies, waits for them, and re-layouts  2.71 us

profile of v1, /device:TPU:0, one launch (start us, length us, event | category | flops | bytes accessed | tf_op | source)
XLA Modules:
  0.0 103.3 jit_solution(14758605253242883083)
XLA Ops:
  0.0 1.3 %copy.8.send_list = s32[1,16,2]{2,1,0:T(8,128)} copy(s32[1,16,2]{1,2,0:T(2,128)} %param.10) | data formatting | bytes 256 | tf_op args[3]
  1.4 1.4 %copy.9.rel_index = s32[24,4]{1,0:T(8,128)} copy(s32[24,4]{0,1:T(4,128)} %param.11) | data formatting | bytes 768 | tf_op args[4]
  2.7 98.0 %shard_map.73 = f32[200,256]{1,0:T(8,128)} custom-call(bf16[3072,3200]{1,0:T(8,128)(2,1)} %geno.1, bf16[3200,256]{1,0:T(8,128)(2,1)} %direc.1, bf16[24,4,128,128]{3,2,1,0:T(8,128)(2,1)} %prec.1, s32[1,16,2]{2,1,0:T(8,128)} %copy.8.send_list, s32[24,4]{1,0:T(8,128)} %copy.9.rel_index, s32[24]{0:T(128)} %rel_count.1), custom_call_target="tpu_custom_call" | custom-call | tf_op jit(solution)/shard_map/pallas_call | solution.py:331
  100.8 0.8 dynamic_slice.6
  101.5 1.8 %multiply_add_fusion = f32[200,256]{1,0:T(8,128)} fusion(f32[200,256]{1,0:T(8,128)} %shard_map.73, bf16[3200,256]{1,0:T(8,128)(2,1)} %direc.1, s32[]{:T(128)S(6)} %select_n.4, f32[200]{0:T(256)S(1)} %dynamic_slice.6), kind=kLoop, calls=%fused_computation | loop fusion | flops 204800 | bytes 512804 | tf_op jit(solution)/shard_map/add | solution.py:376

commit v2 on v0

v2 whole, which is shorter than its diff:
```python
import math

import jax
import jax.numpy as jnp
from jax import lax
from jax.experimental import pallas as pl
from jax.experimental.pallas import tpu as pltpu
from jax.sharding import PartitionSpec as P

MESH = pl.DeviceIdType.MESH
MARKERS = 25600
ANIMALS = 49152
BLK = 128
K = 256
HALF = 128
NB = 24
NREL = 4
PEERS = 16
SLOTS = 2
ROWS = NB * BLK
COLS = 3200
OWN = 200
KO = 16
CB = 4
W = CB * BLK
NC = NB // CB
NI = 2 * NC
F32 = jnp.float32
BF16 = jnp.bfloat16


def kernel(
    geno, direc, prec, send_hbm, index_hbm, rel_count, out,
    g_v, d_v, prec_v, send_list, rel_index, st, r1p, r1m, r2p, r2m, ry, t_loc, table0, table1, stage, rt, ot, o_full, cx,
    d1, d2p, d2m, dy, e1p, e1m, e2p, e2m, ey,
    ld_sem, ldg_sem, a_send, a_recv, b_send, b_recv, c_send, c_recv, x_send, x_recv, d_send, d_recv,
):
    a = lax.axis_index("animal")
    m = lax.axis_index("marker")
    z, yh = m // 2, m % 2
    zp, zm, zo = (z + 1) % 4, (z + 3) % 4, (z + 2) % 4
    up, down, across = zp * 2 + yh, zm * 2 + yh, z * 2 + 1 - yh
    yl, x, core = a // 8, (a // 2) % 4, a % 2
    xp, xm, xo = (x + 1) % 4, (x + 3) % 4, (x + 2) % 4
    right, left = yl * 8 + xp * 2 + core, yl * 8 + xm * 2 + core
    beside, sibling = (1 - yl) * 8 + x * 2 + core, yl * 8 + x * 2 + 1 - core

    tables = (table0, table1)

    def load_g(c):
        rows = pl.ds(pl.multiple_of(c * W, W), W)
        return pltpu.make_async_copy(geno.at[rows], g_v.at[rows], ldg_sem.at[c])

    load_d = pltpu.make_async_copy(direc, d_v, ld_sem.at[0])
    load_p = pltpu.make_async_copy(prec, prec_v, ld_sem.at[1])
    load_s = pltpu.make_async_copy(send_hbm, send_list, ld_sem.at[2])
    load_i = pltpu.make_async_copy(index_hbm, rel_index, ld_sem.at[3])

    def remote(src, dst, send, recv, **device):
        return pltpu.make_async_remote_copy(
            src_ref=src, dst_ref=dst, send_sem=send, recv_sem=recv, device_id=device, device_id_type=MESH
        )

    load_d.start()
    load_g(0).start()
    load_g(1).start()
    barrier = pltpu.get_barrier_semaphore()

    def greet(i, carry):
        pl.semaphore_signal(barrier, inc=1, device_id={"animal": (a + i) % PEERS}, device_id_type=MESH)
        return carry

    lax.fori_loop(1, PEERS, greet, 0)
    for other in (up, down, across):
        pl.semaphore_signal(barrier, inc=1, device_id={"marker": other}, device_id_type=MESH)
    load_s.start()
    load_i.start()
    load_d.wait()

    def krows(i, start, size):
        return pl.ds(pl.multiple_of((i // NC) * HALF + start, KO), size)

    def a1p(i):
        return remote(st.at[i % NC, krows(i, zo * 32, KO)], r1p.at[i], a_send.at[0, i], a_recv.at[0, i], marker=up)

    def a1m(i):
        return remote(st.at[i % NC, krows(i, zo * 32 + KO, KO)], r1m.at[i], a_send.at[1, i], a_recv.at[1, i], marker=down)

    def a2p(i):
        return remote(st.at[i % NC, krows(i, zp * 32, 32)], r2p.at[i], a_send.at[2, i], a_recv.at[2, i], marker=up)

    def a2m(i):
        return remote(st.at[i % NC, krows(i, zm * 32, 32)], r2m.at[i], a_send.at[3, i], a_recv.at[3, i], marker=down)

    def ay(i):
        rows = krows(i, z * 32 + (1 - yh) * KO, KO)
        return remote(st.at[i % NC, rows], ry.at[i], a_send.at[4, i], a_recv.at[4, i], marker=across)

    def product(c):
        load_g(c).wait()
        rows = pl.ds(pl.multiple_of(c * W, W), W)
        st[c] = jnp.dot(g_v[rows, :], d_v[...], preferred_element_type=F32).T

    def reduce1(i):
        a1p(i).start()
        a1m(i).start()

    def reduce2(i):
        a1p(i).wait_recv()
        near = krows(i, zp * 32, KO)
        st[i % NC, near] = st[i % NC, near] + r1p[i]
        a2p(i).start()
        a1m(i).wait_recv()
        near = krows(i, zm * 32 + KO, KO)
        st[i % NC, near] = st[i % NC, near] + r1m[i]
        a2m(i).start()

    def reduce3(i):
        a2p(i).wait_recv()
        a2m(i).wait_recv()
        own = krows(i, z * 32, 32)
        st[i % NC, own] = st[i % NC, own] + (r2p[i] + r2m[i])
        ay(i).start()

    def reduce4(i, h):
        ay(i).wait_recv()
        done = st[i % NC, krows(i, z * 32 + yh * KO, KO)] + ry[i]
        done = (done * (1.0 / math.sqrt(MARKERS))).astype(BF16)
        for b in range(CB):
            t_loc[h, (i % NC) * CB + b] = done[:, b * BLK : (b + 1) * BLK]
            tables[h][(i % NC) * CB + b] = done[:, b * BLK : (b + 1) * BLK]

    def drain_a(i, carry):
        for copy in (a1p, a1m, a2p, a2m, ay):
            copy(i).wait_send()
        return carry

    def b_copy(h, e, p):
        return remote(
            stage.at[h, e], tables[h].at[pl.ds(NB + SLOTS * p, SLOTS)], b_send.at[h, e], b_recv.at[h, p], animal=e
        )

    def relatives_out(h):
        def one(i, carry):
            e = (a + i) % PEERS
            for s in range(SLOTS):
                stage[h, e, s] = t_loc[h, send_list[0, e, s]]
            b_copy(h, e, a).start()
            return carry

        lax.fori_loop(1, PEERS, one, 0)
        for s in range(SLOTS):
            tables[h][NB + SLOTS * a + s] = t_loc[h, send_list[0, a, s]]

    def relatives_in(h):
        def one(i, carry):
            p = (a + i) % PEERS
            b_copy(h, p, p).wait_recv()
            return carry

        lax.fori_loop(1, PEERS, one, 0)

    def drain_b(h):
        def one(i, carry):
            b_copy(h, (a + i) % PEERS, a).wait_send()
            return carry

        lax.fori_loop(1, PEERS, one, 0)

    def c_copy(kind, i, owner, to):
        rows = krows(i, owner * KO, KO)
        return remote(
            rt.at[i % NC, rows], rt.at[i % NC, rows], c_send.at[kind, i], c_recv.at[kind, i], marker=to
        )

    def arrived(kind, i):
        owner = (across, down, up, zm * 2 + 1 - yh, zp * 2 + 1 - yh, zo * 2 + yh, zo * 2 + 1 - yh)[kind]
        c_copy(kind, i, owner, up).wait_recv()

    def relative_sums(h):
        def one(c, carry):
            i = h * NC + c
            for b in range(CB):
                g = c * CB + b
                count = rel_count[g]
                picked = []
                for j in range(NREL):
                    block = tables[h][rel_index[g, j]]
                    picked.append(jnp.where(j < count, block, jnp.zeros_like(block)))
                total = lax.dot_general(
                    jnp.concatenate(picked, axis=1),
                    jnp.concatenate([prec_v[g, j] for j in range(NREL)], axis=1),
                    (((1,), (1,)), ((), ())),
                    preferred_element_type=F32,
                )
                rt[c, krows(i, m * KO, KO), b * BLK : (b + 1) * BLK] = total.astype(BF16)
            c_copy(1, i, m, up).start()
            c_copy(2, i, m, down).start()
            c_copy(0, i, m, across).start()
            return carry

        lax.fori_loop(0, NC, one, 0)

    def gather_y(i):
        arrived(0, i)
        c_copy(3, i, across, up).start()
        c_copy(4, i, across, down).start()

    def gather_relay(i):
        arrived(1, i)
        c_copy(5, i, down, up).start()
        arrived(4, i)
        c_copy(6, i, zp * 2 + 1 - yh, down).start()

    def drain_c(i, carry):
        for kind in range(7):
            c_copy(kind, i, m, up).wait_send()
        return carry

    def marker_part(h, c):
        i = h * NC + c
        for kind in (2, 3, 5, 6):
            arrived(kind, i)
        rows = pl.ds(pl.multiple_of(c * W, W), W)
        return jnp.dot(rt[c, h * HALF : (h + 1) * HALF], g_v[rows, :], preferred_element_type=F32)

    def marker_first(h):
        ot[...] = marker_part(h, 0)

    def marker_next(h, c):
        ot[...] = ot[...] + marker_part(h, c)

    def marker_last(h):
        o_full[h] = (ot[...] + marker_part(h, NC - 1)).T

    def owner_rows(q, side):
        return pl.ds(pl.multiple_of((2 * q + side) * OWN, 8), OWN)

    def x_copy(h, q):
        return remote(
            o_full.at[h, owner_rows(q, 1 - core)], cx.at[h, q], x_send.at[h, q], x_recv.at[h, q], animal=sibling
        )

    def cores_out(h):
        for q in (xo, 4 + xo, 4 + xp, xm, xp, 4 + xm, x, 4 + x):
            x_copy(h, q).start()

    def chip_sum(h, q):
        x_copy(h, q).wait_recv()
        return o_full[h, owner_rows(q, core)] + cx[h, q]

    def d_copy(h, kind):
        src, dst, to = (
            (d1.at[h, 0], e1p.at[h], right), (d1.at[h, 1], e1m.at[h], left),
            (d2p.at[h, 0], e2p.at[h, 0], right), (d2p.at[h, 1], e2p.at[h, 1], right),
            (d2m.at[h, 0], e2m.at[h, 0], left), (d2m.at[h, 1], e2m.at[h, 1], left),
            (dy.at[h], ey.at[h], beside),
        )[kind]
        return remote(src, dst, d_send.at[h, kind], d_recv.at[h, kind], animal=to)

    def ring1(h):
        d1[h, 0] = chip_sum(h, xo).astype(BF16)
        d_copy(h, 0).start()
        d1[h, 1] = chip_sum(h, 4 + xo).astype(BF16)
        d_copy(h, 1).start()
        d2p[h, 1] = chip_sum(h, 4 + xp).astype(BF16)
        d_copy(h, 3).start()
        d2m[h, 0] = chip_sum(h, xm).astype(BF16)
        d_copy(h, 4).start()

    def ring2(h):
        near = chip_sum(h, xp)
        d_copy(h, 0).wait_recv()
        d2p[h, 0] = (near + e1p[h].astype(F32)).astype(BF16)
        d_copy(h, 2).start()
        near = chip_sum(h, 4 + xm)
        d_copy(h, 1).wait_recv()
        d2m[h, 1] = (near + e1m[h].astype(F32)).astype(BF16)
        d_copy(h, 5).start()

    def ring_sum(h, side):
        q = side * 4 + x
        own = o_full[h, owner_rows(q, core)] + cx[h, q]
        return own + e2p[h, side].astype(F32) + e2m[h, side].astype(F32)

    def ring3(h):
        x_copy(h, x).wait_recv()
        x_copy(h, 4 + x).wait_recv()
        for kind in (2, 3, 4, 5):
            d_copy(h, kind).wait_recv()
        dy[h] = ring_sum(h, 1 - yl).astype(BF16)
        d_copy(h, 6).start()

    def finish(h):
        mine = ring_sum(h, yl)
        d_copy(h, 6).wait_recv()
        out[:, h * HALF : (h + 1) * HALF] = mine + ey[h].astype(F32)

    def drain_d(h):
        for q in range(8):
            x_copy(h, q).wait_send()
        for kind in range(7):
            d_copy(h, kind).wait_send()

    def each(count, step):
        def one(i, carry):
            step(i)
            return carry

        lax.fori_loop(0, count, one, 0)

    def step_a(it):
        @pl.when(it < NC)
        def _():
            @pl.when(it + 2 < NC)
            def _():
                load_g(it + 2).start()

            @pl.when(it == NC - 1)
            def _():
                load_p.start()

            product(it)

            @pl.when(it == 0)
            def _():
                pl.semaphore_wait(barrier, PEERS - 1 + 3)

        reduce1(it)
        pl.when(it >= 1)(lambda: reduce2(it - 1))
        pl.when(it >= 2)(lambda: reduce3(it - 2))
        pl.when(it >= 3)(lambda: reduce4(it - 3, 0))

    each(NC + 3, step_a)
    load_s.wait()
    load_i.wait()
    relatives_out(0)

    def step_a2(j):
        it = NC + 3 + j
        reduce1(it)
        reduce2(it - 1)
        reduce3(it - 2)
        reduce4(it - 3, 1)

    each(NI - NC - 3, step_a2)
    load_p.wait()
    relatives_in(0)
    relative_sums(0)
    reduce2(NI - 1)
    reduce3(NI - 2)
    reduce4(NI - 3, 1)
    reduce3(NI - 1)
    reduce4(NI - 2, 1)
    each(NC, gather_y)
    reduce4(NI - 1, 1)
    relatives_out(1)
    each(NC, gather_relay)
    relatives_in(1)
    relative_sums(1)
    marker_first(0)

    def middle(c):
        marker_next(0, c + 1)
        gather_y(NC + c)

    each(NC - 2, middle)
    gather_y(NI - 2)
    gather_y(NI - 1)
    marker_last(0)
    cores_out(0)
    each(NC, lambda c: gather_relay(NC + c))
    ring1(0)
    marker_first(1)
    marker_next(1, 1)
    ring2(0)
    each(2, lambda c: marker_next(1, c + 2))
    ring3(0)
    marker_next(1, NC - 2)
    marker_last(1)
    cores_out(1)
    finish(0)
    ring1(1)
    ring2(1)
    ring3(1)
    finish(1)

    lax.fori_loop(0, NI, drain_a, 0)
    lax.fori_loop(0, NI, drain_c, 0)
    for h in range(2):
        drain_b(h)
        drain_d(h)


def local(genotypes, direction, ridge, send_list, rel_index, rel_count, rel_prec):
    hbm = pl.BlockSpec(memory_space=pl.ANY)
    smem = pl.BlockSpec(memory_space=pltpu.SMEM)
    vmem = pl.BlockSpec(memory_space=pltpu.VMEM)
    dma = pltpu.SemaphoreType.DMA
    gradient = pl.pallas_call(
        kernel,
        out_shape=jax.ShapeDtypeStruct((OWN, K), F32),
        in_specs=[hbm, hbm, hbm, hbm, hbm, smem],
        out_specs=vmem,
        scratch_shapes=[
            pltpu.VMEM((ROWS, COLS), BF16),
            pltpu.VMEM((COLS, K), BF16),
            pltpu.VMEM((NB, NREL, BLK, BLK), BF16),
            pltpu.SMEM((1, PEERS, SLOTS), jnp.int32),
            pltpu.SMEM((NB, NREL), jnp.int32),
            pltpu.VMEM((NC, K, W), F32),
            pltpu.VMEM((NI, KO, W), F32),
            pltpu.VMEM((NI, KO, W), F32),
            pltpu.VMEM((NI, 2 * KO, W), F32),
            pltpu.VMEM((NI, 2 * KO, W), F32),
            pltpu.VMEM((NI, KO, W), F32),
            pltpu.VMEM((2, NB, KO, BLK), BF16),
            pltpu.VMEM((NB + PEERS * SLOTS, KO, BLK), BF16),
            pltpu.VMEM((NB + PEERS * SLOTS, KO, BLK), BF16),
            pltpu.VMEM((2, PEERS, SLOTS, KO, BLK), BF16),
            pltpu.VMEM((NC, K, W), BF16),
            pltpu.VMEM((HALF, COLS), F32),
            pltpu.VMEM((2, COLS, HALF), F32),
            pltpu.VMEM((2, 8, OWN, HALF), F32),
            pltpu.VMEM((2, 2, OWN, HALF), BF16),
            pltpu.VMEM((2, 2, OWN, HALF), BF16),
            pltpu.VMEM((2, 2, OWN, HALF), BF16),
            pltpu.VMEM((2, OWN, HALF), BF16),
            pltpu.VMEM((2, OWN, HALF), BF16),
            pltpu.VMEM((2, OWN, HALF), BF16),
            pltpu.VMEM((2, 2, OWN, HALF), BF16),
            pltpu.VMEM((2, 2, OWN, HALF), BF16),
            pltpu.VMEM((2, OWN, HALF), BF16),
            dma((4,)), dma((NC,)),
            dma((5, NI)), dma((5, NI)),
            dma((2, PEERS)), dma((2, PEERS)),
            dma((7, NI)), dma((7, NI)),
            dma((2, 8)), dma((2, 8)),
            dma((2, 7)), dma((2, 7)),
        ],
        compiler_params=pltpu.CompilerParams(
            collective_id=0, has_side_effects=True, vmem_limit_bytes=63000000
        ),
    )(genotypes, direction, rel_prec, send_list, rel_index, rel_count)
    row_start = lax.axis_index("animal") * OWN
    own_ridge = lax.dynamic_slice_in_dim(ridge, row_start, OWN, 0)
    own_direction = lax.dynamic_slice_in_dim(direction, row_start, OWN, 0)
    return gradient * (1.0 / math.sqrt(ANIMALS)) + own_ridge[:, None] * own_direction.astype(F32)


def solution(mesh):
    in_specs = (
        P("animal", "marker"),
        P("marker", None),
        P("marker"),
        P("animal", None, None),
        P("animal", None),
        P("animal"),
        P("animal", None, None, None),
    )
    out_specs = P(("marker", "animal"), None)
    return jax.shard_map(local, mesh=mesh, in_specs=in_specs, out_specs=out_specs, check_vma=False)
```

time: 314 us -> 99.2 us (0.32)
  waiting for transfers between devices: 239 us -> 0 us
  Pallas kernels: 0 us -> 93.7 us
  matrix products: 26.5 us -> 0 us
  local copies, waits for them, and re-layouts: 21.9 us -> 3.48 us
  between operations: 13.5 us -> 0.02 us
  other arithmetic: 8.45 us -> 1.77 us
  starting transfers between devices: 4.62 us -> 0 us
    psum x1 -> x0, waiting for transfers between devices: 148 us -> none  [local(): summed = lax.psum(partial_value, 'marker')]
    pallas_call x0 -> x1, Pallas kernels: none -> 93.7 us  [local(): pl.pallas_call(kernel, out_shape=jax.ShapeDtypeStruct((OWN, K), F32), in_...]
    unnamed x3 -> x0, waiting for transfers between devices: 63 us -> none
    all_to_all x1 -> x0, waiting for transfers between devices: 27.7 us -> none  [pedigree(): lax.all_to_all(outgoing, 'animal', split_axis=0, concat_axis=0, tiled=True)]
    dot_general x3 -> x0, matrix products: 26.5 us -> none  [the longest x1 11.2 us: local(): lax.dot_general(genotypes, effects, (((0,), (0,)), ((), ())), preferred_e...]
    gather x2 -> x0, local copies, waits for them, and re-layouts: 11.4 us -> none  [the longest x1 8.05 us: pedigree(): gathered = source_table[rel_index]]
    all_to_all x1 -> x0, starting transfers between devices: 4.58 us -> none  [pedigree(): lax.all_to_all(outgoing, 'animal', split_axis=0, concat_axis=0, tiled=True)]
    concatenate x1 -> x0, other arithmetic: 4.22 us -> none  [pedigree(): jnp.concatenate([blocked, incoming.reshape(-1, BLK, col_total)], axis=0)]
  transfers between devices with their start and end apart: 3 -> 0, of which waited for: 3 -> 0; matrix products, arithmetic and copies ran while one was open for 1% -> 0% of each run, Pallas kernels for 0% -> 0%
where the time goes in v2:
time: 99.2 us; the launch traced here: 98.9 us
  Pallas kernels  93.7 us (94%)
  local copies, waits for them, and re-layouts  3.48 us (4%)
  other arithmetic  1.77 us (2%)
    pallas_call x1, Pallas kernels, local(): pl.pallas_call(kernel, out_shape=jax.ShapeDtypeStruct((OWN, K), F32), in_...  93.7 us
    unnamed x2, local copies, waits for them, and re-layouts  2.71 us

profile of v2, /device:TPU:0, one launch (start us, length us, event | category | flops | bytes accessed | tf_op | source)
XLA Modules:
  0.0 98.9 jit_solution(3611680938043769232)
XLA Ops:
  0.0 1.3 %copy.8.send_hbm = s32[1,16,2]{2,1,0:T(8,128)} copy(s32[1,16,2]{1,2,0:T(2,128)} %param.10) | data formatting | bytes 256 | tf_op args[3]
  1.4 1.4 %copy.9.index_hbm = s32[24,4]{1,0:T(8,128)} copy(s32[24,4]{0,1:T(4,128)} %param.11) | data formatting | bytes 768 | tf_op args[4]
  2.7 93.7 %shard_map.73 = f32[200,256]{1,0:T(8,128)} custom-call(bf16[3072,3200]{1,0:T(8,128)(2,1)} %geno.1, bf16[3200,256]{1,0:T(8,128)(2,1)} %direc.1, bf16[24,4,128,128]{3,2,1,0:T(8,128)(2,1)} %prec.1, s32[1,16,2]{2,1,0:T(8,128)} %copy.8.send_hbm, s32[24,4]{1,0:T(8,128)} %copy.9.index_hbm, s32[24]{0:T(128)} %rel_count.1), custom_call_target="tpu_custom_call" | custom-call | tf_op jit(solution)/shard_map/pallas_call | solution.py:400
  96.4 0.8 dynamic_slice.6
  97.2 1.8 %multiply_add_fusion = f32[200,256]{1,0:T(8,128)} fusion(f32[200,256]{1,0:T(8,128)} %shard_map.73, bf16[3200,256]{1,0:T(8,128)(2,1)} %direc.1, s32[]{:T(128)S(6)} %select_n.4, f32[200]{0:T(256)S(1)} %dynamic_slice.6), kind=kLoop, calls=%fused_computation | loop fusion | flops 204800 | bytes 512804 | tf_op jit(solution)/shard_map/add | solution.py:448

commit v3 on v2

v3 whole, which is shorter than its diff:
```python
import math

import jax
import jax.numpy as jnp
from jax import lax
from jax.experimental import pallas as pl
from jax.experimental.pallas import tpu as pltpu
from jax.sharding import PartitionSpec as P

MESH = pl.DeviceIdType.MESH
MARKERS = 25600
ANIMALS = 49152
BLK = 128
K = 256
HALF = 128
NB = 24
NREL = 4
PEERS = 16
SLOTS = 2
ROWS = NB * BLK
COLS = 3200
OWN = 200
KO = 16
CB = 4
W = CB * BLK
NC = NB // CB
NI = 2 * NC
AWAY = ((1, 2), (0, 2), (1, 1), (1, 3), (0, 1), (0, 3), (1, 0))
F32 = jnp.float32
BF16 = jnp.bfloat16


def kernel(
    geno, direc, own_direc, ridge, prec, send_hbm, index_hbm, rel_count, out,
    g_v, d_v, own_v, ridge_v, ridge_col, prec_v, send_list, rel_index, st, r1p, r1m, r2p, r2m, ry, t_loc, table0, table1, stage, rt, ot, o_full, cx,
    d_out, d_in,
    ld_sem, ldg_sem, a_send, a_recv, b_send, b_recv, c_send, c_recv, x_send, x_recv, d_send, d_recv,
):
    a = lax.axis_index("animal")
    m = lax.axis_index("marker")
    z, yh = m // 2, m % 2
    zp, zm, zo = (z + 1) % 4, (z + 3) % 4, (z + 2) % 4
    up, down, across = zp * 2 + yh, zm * 2 + yh, z * 2 + 1 - yh
    core, mine = a % 2, a // 2
    yl, x = mine // 4, mine % 4
    sibling = 2 * mine + 1 - core
    markers_away = [((z + dz) % 4 * 2 + (yh + dy) % 2, (z + 4 - dz) % 4 * 2 + (yh + dy) % 2) for dy, dz in AWAY]
    animals_away = [(yl + dy) % 2 * 4 + (x + dx) % 4 for dy, dx in AWAY]
    tables = (table0, table1)

    def load_g(c):
        rows = pl.ds(pl.multiple_of(c * W, W), W)
        return pltpu.make_async_copy(geno.at[rows], g_v.at[rows], ldg_sem.at[c])

    load_d = pltpu.make_async_copy(direc, d_v, ld_sem.at[0])
    load_p = pltpu.make_async_copy(prec, prec_v, ld_sem.at[1])
    load_s = pltpu.make_async_copy(send_hbm, send_list, ld_sem.at[2])
    load_i = pltpu.make_async_copy(index_hbm, rel_index, ld_sem.at[3])
    load_o = pltpu.make_async_copy(own_direc.at[a], own_v, ld_sem.at[4])
    load_r = pltpu.make_async_copy(ridge, ridge_v, ld_sem.at[5])

    def remote(src, dst, send, recv, **device):
        return pltpu.make_async_remote_copy(
            src_ref=src, dst_ref=dst, send_sem=send, recv_sem=recv, device_id=device, device_id_type=MESH
        )

    load_d.start()
    load_g(0).start()
    load_g(1).start()
    barrier = pltpu.get_barrier_semaphore()

    def greet(i, carry):
        pl.semaphore_signal(barrier, inc=1, device_id={"animal": (a + i) % PEERS}, device_id_type=MESH)
        return carry

    lax.fori_loop(1, PEERS, greet, 0)
    for other, _ in markers_away:
        pl.semaphore_signal(barrier, inc=1, device_id={"marker": other}, device_id_type=MESH)
    load_s.start()
    load_i.start()
    load_o.start()
    load_r.start()
    load_d.wait()

    def krows(i, start, size):
        return pl.ds(pl.multiple_of((i // NC) * HALF + start, KO), size)

    def a1p(i):
        return remote(st.at[i % NC, krows(i, zo * 32, KO)], r1p.at[i], a_send.at[0, i], a_recv.at[0, i], marker=up)

    def a1m(i):
        return remote(st.at[i % NC, krows(i, zo * 32 + KO, KO)], r1m.at[i], a_send.at[1, i], a_recv.at[1, i], marker=down)

    def a2p(i):
        return remote(st.at[i % NC, krows(i, zp * 32, 32)], r2p.at[i], a_send.at[2, i], a_recv.at[2, i], marker=up)

    def a2m(i):
        return remote(st.at[i % NC, krows(i, zm * 32, 32)], r2m.at[i], a_send.at[3, i], a_recv.at[3, i], marker=down)

    def ay(i):
        rows = krows(i, z * 32 + (1 - yh) * KO, KO)
        return remote(st.at[i % NC, rows], ry.at[i], a_send.at[4, i], a_recv.at[4, i], marker=across)

    def product(c):
        load_g(c).wait()
        rows = pl.ds(pl.multiple_of(c * W, W), W)
        st[c] = jnp.dot(g_v[rows, :], d_v[...], preferred_element_type=F32).T

    def reduce1(i):
        a1p(i).start()
        a1m(i).start()

    def reduce2(i):
        a1p(i).wait_recv()
        near = krows(i, zp * 32, KO)
        st[i % NC, near] = st[i % NC, near] + r1p[i]
        a2p(i).start()
        a1m(i).wait_recv()
        near = krows(i, zm * 32 + KO, KO)
        st[i % NC, near] = st[i % NC, near] + r1m[i]
        a2m(i).start()

    def reduce3(i):
        a2p(i).wait_recv()
        a2m(i).wait_recv()
        own = krows(i, z * 32, 32)
        st[i % NC, own] = st[i % NC, own] + (r2p[i] + r2m[i])
        ay(i).start()

    def reduce4(i, h):
        ay(i).wait_recv()
        done = st[i % NC, krows(i, z * 32 + yh * KO, KO)] + ry[i]
        done = (done * (1.0 / math.sqrt(MARKERS))).astype(BF16)
        for b in range(CB):
            t_loc[h, (i % NC) * CB + b] = done[:, b * BLK : (b + 1) * BLK]
            tables[h][(i % NC) * CB + b] = done[:, b * BLK : (b + 1) * BLK]

    def drain_a(i, carry):
        for copy in (a1p, a1m, a2p, a2m, ay):
            copy(i).wait_send()
        return carry

    def b_copy(h, e, p):
        return remote(
            stage.at[h, e], tables[h].at[pl.ds(NB + SLOTS * p, SLOTS)], b_send.at[h, e], b_recv.at[h, p], animal=e
        )

    def relatives_out(h):
        for i in range(1, PEERS):
            e = (a + i) % PEERS
            for s in range(SLOTS):
                stage[h, e, s] = t_loc[h, send_list[s, e]]
            b_copy(h, e, a).start()
        for s in range(SLOTS):
            tables[h][NB + SLOTS * a + s] = t_loc[h, send_list[s, a]]

    def relatives_in(h):
        def one(i, carry):
            p = (a + i) % PEERS
            b_copy(h, p, p).wait_recv()
            return carry

        lax.fori_loop(1, PEERS, one, 0)

    def drain_b(h):
        def one(i, carry):
            b_copy(h, (a + i) % PEERS, a).wait_send()
            return carry

        lax.fori_loop(1, PEERS, one, 0)

    def c_copy(kind, i, owner):
        rows = krows(i, owner * KO, KO)
        to = markers_away[kind][0]
        return remote(rt.at[i % NC, rows], rt.at[i % NC, rows], c_send.at[kind, i], c_recv.at[kind, i], marker=to)

    def relative_sums(h):
        def one(c, carry):
            i = h * NC + c
            for b in range(CB):
                g = c * CB + b
                count = rel_count[g]
                picked = []
                for j in range(NREL):
                    block = tables[h][rel_index[j, g]]
                    picked.append(jnp.where(j < count, block, jnp.zeros_like(block)))
                total = lax.dot_general(
                    jnp.concatenate(picked, axis=1),
                    jnp.concatenate([prec_v[g, j] for j in range(NREL)], axis=1),
                    (((1,), (1,)), ((), ())),
                    preferred_element_type=F32,
                )
                rt[c, krows(i, m * KO, KO), b * BLK : (b + 1) * BLK] = total.astype(BF16)
            for kind in range(7):
                c_copy(kind, i, m).start()
            return carry

        lax.fori_loop(0, NC, one, 0)

    def drain_c(i, carry):
        for kind in range(7):
            c_copy(kind, i, m).wait_send()
        return carry

    def gather_end(h, c):
        for kind in range(7):
            c_copy(kind, h * NC + c, markers_away[kind][1]).wait_recv()

    def marker_part(h, c):
        rows = pl.ds(pl.multiple_of(c * W, W), W)
        return jnp.dot(rt[c, h * HALF : (h + 1) * HALF], g_v[rows, :], preferred_element_type=F32)

    def marker_first(h):
        ot[...] = marker_part(h, 0)

    def marker_next(h, c):
        ot[...] = ot[...] + marker_part(h, c)

    def marker_last(h):
        o_full[h] = (ot[...] + marker_part(h, NC - 1)).T

    def owner_rows(q, side):
        return pl.ds(pl.multiple_of((2 * q + side) * OWN, 8), OWN)

    def x_copy(h, q):
        return remote(
            o_full.at[h, owner_rows(q, 1 - core)], cx.at[h, q], x_send.at[h, q], x_recv.at[h, q], animal=sibling
        )

    def d_copy(h, q, sender):
        return remote(d_out.at[h, q], d_in.at[h, sender], d_send.at[h, q], d_recv.at[h, sender], animal=2 * q + core)

    def cores_out(h):
        for q in animals_away + [mine]:
            x_copy(h, q).start()

    def chip_sum(h, q):
        x_copy(h, q).wait_recv()
        return o_full[h, owner_rows(q, core)] + cx[h, q]

    def owners_out(h):
        for q in animals_away:
            d_out[h, q] = chip_sum(h, q).astype(BF16)
            d_copy(h, q, mine).start()

    def ridge_column():
        load_r.wait()
        turned = ridge_v[...].T
        for j in range(COLS // BLK):
            ridge_col[j * BLK : (j + 1) * BLK] = turned[:, j : j + 1]

    def finish(h):
        cols = slice(h * HALF, (h + 1) * HALF)
        own = pl.ds(pl.multiple_of(a * OWN, 8), OWN)
        total = chip_sum(h, mine)
        for q in animals_away:
            d_copy(h, q, q).wait_recv()
            total = total + d_in[h, q].astype(F32)
        out[:, cols] = total * (1.0 / math.sqrt(ANIMALS)) + ridge_col[own] * own_v[:, cols].astype(F32)

    def drain_d(h):
        for q in animals_away:
            x_copy(h, q).wait_send()
            d_copy(h, q, mine).wait_send()
        x_copy(h, mine).wait_send()

    def each(count, step):
        def one(i, carry):
            step(i)
            return carry

        lax.fori_loop(0, count, one, 0)

    def step_a(it):
        @pl.when(it < NC)
        def _():
            @pl.when(it + 2 < NC)
            def _():
                load_g(it + 2).start()

            @pl.when(it == NC - 1)
            def _():
                load_p.start()

            product(it)

            @pl.when(it == 0)
            def _():
                pl.semaphore_wait(barrier, PEERS - 1 + len(AWAY))

        reduce1(it)
        pl.when(it >= 2)(lambda: reduce2(it - 2))
        pl.when(it >= 4)(lambda: reduce3(it - 4))
        pl.when(it >= 6)(lambda: reduce4(it - 6, 0))

    each(NI, step_a)
    load_s.wait()
    load_i.wait()
    relatives_out(0)
    for i in (NI - 2, NI - 1):
        reduce2(i)
        reduce3(i - 2)
        reduce4(i - 4, 1)
    ridge_column()
    load_o.wait()
    for i in (NI - 2, NI - 1):
        reduce3(i)
        reduce4(i - 2, 1)
    load_p.wait()
    relatives_in(0)
    relative_sums(0)
    reduce4(NI - 2, 1)
    reduce4(NI - 1, 1)
    relatives_out(1)
    relatives_in(1)
    relative_sums(1)

    def step_m(h, c):
        gather_end(h, c)
        marker_next(h, c)

    gather_end(0, 0)
    marker_first(0)
    each(NC - 2, lambda c: step_m(0, c + 1))
    gather_end(0, NC - 1)
    marker_last(0)
    cores_out(0)
    gather_end(1, 0)
    marker_first(1)
    step_m(1, 1)
    owners_out(0)
    each(NC - 3, lambda c: step_m(1, c + 2))
    gather_end(1, NC - 1)
    marker_last(1)
    cores_out(1)
    finish(0)
    owners_out(1)
    finish(1)

    lax.fori_loop(0, NI, drain_a, 0)
    lax.fori_loop(0, NI, drain_c, 0)
    for h in range(2):
        drain_b(h)
        drain_d(h)


def local(genotypes, direction, ridge, send_list, rel_index, rel_count, rel_prec):
    hbm = pl.BlockSpec(memory_space=pl.ANY)
    smem = pl.BlockSpec(memory_space=pltpu.SMEM)
    vmem = pl.BlockSpec(memory_space=pltpu.VMEM)
    dma = pltpu.SemaphoreType.DMA
    return pl.pallas_call(
        kernel,
        out_shape=jax.ShapeDtypeStruct((OWN, K), F32),
        in_specs=[hbm, hbm, hbm, hbm, hbm, hbm, hbm, smem],
        out_specs=vmem,
        scratch_shapes=[
            pltpu.VMEM((ROWS, COLS), BF16),
            pltpu.VMEM((COLS, K), BF16),
            pltpu.VMEM((OWN, K), BF16),
            pltpu.VMEM((COLS // BLK, BLK), F32),
            pltpu.VMEM((COLS, 1), F32),
            pltpu.VMEM((NB, NREL, BLK, BLK), BF16),
            pltpu.SMEM((SLOTS, PEERS), jnp.int32),
            pltpu.SMEM((NREL, NB), jnp.int32),
            pltpu.VMEM((NC, K, W), F32),
            pltpu.VMEM((NI, KO, W), F32),
            pltpu.VMEM((NI, KO, W), F32),
            pltpu.VMEM((NI, 2 * KO, W), F32),
            pltpu.VMEM((NI, 2 * KO, W), F32),
            pltpu.VMEM((NI, KO, W), F32),
            pltpu.VMEM((2, NB, KO, BLK), BF16),
            pltpu.VMEM((NB + PEERS * SLOTS, KO, BLK), BF16),
            pltpu.VMEM((NB + PEERS * SLOTS, KO, BLK), BF16),
            pltpu.VMEM((2, PEERS, SLOTS, KO, BLK), BF16),
            pltpu.VMEM((NC, K, W), BF16),
            pltpu.VMEM((HALF, COLS), F32),
            pltpu.VMEM((2, COLS, HALF), F32),
            pltpu.VMEM((2, 8, OWN, HALF), F32),
            pltpu.VMEM((2, 8, OWN, HALF), BF16),
            pltpu.VMEM((2, 8, OWN, HALF), BF16),
            dma((6,)), dma((NC,)),
            dma((5, NI)), dma((5, NI)),
            dma((2, PEERS)), dma((2, PEERS)),
            dma((7, NI)), dma((7, NI)),
            dma((2, 8)), dma((2, 8)),
            dma((2, 8)), dma((2, 8)),
        ],
        compiler_params=pltpu.CompilerParams(
            collective_id=0, has_side_effects=True, vmem_limit_bytes=63000000
        ),
    )(
        genotypes,
        direction,
        direction.reshape(PEERS, OWN, K),
        ridge.reshape(COLS // BLK, BLK),
        rel_prec,
        send_list[0].T,
        rel_index.T,
        rel_count,
    )


def solution(mesh):
    in_specs = (
        P("animal", "marker"),
        P("marker", None),
        P("marker"),
        P("animal", None, None),
        P("animal", None),
        P("animal"),
        P("animal", None, None, None),
    )
    out_specs = P(("marker", "animal"), None)
    return jax.shard_map(local, mesh=mesh, in_specs=in_specs, out_specs=out_specs, check_vma=False)
```

time: 99.2 us -> 82 us (0.83)
  Pallas kernels: 93.7 us -> 79.2 us
  local copies, waits for them, and re-layouts: 3.48 us -> 1.62 us
  other arithmetic: 1.77 us -> 0 us
    pallas_call x1, Pallas kernels: 93.7 us -> 79.2 us  [local(): pl.pallas_call(kernel, out_shape=jax.ShapeDtypeStruct((OWN, K), F32), in_...]
    add x1 -> x0, other arithmetic: 1.77 us -> none  [local(): gradient * (1.0 / math.sqrt(ANIMALS))]
    unnamed x2 -> x1, local copies, waits for them, and re-layouts: 2.71 us -> 1.62 us
where the time goes in v3:
time: 82 us; the launch traced here: 80.8 us
  Pallas kernels  79.2 us (97%)
  local copies, waits for them, and re-layouts  1.62 us (2%)
    pallas_call x1, Pallas kernels, local(): pl.pallas_call(kernel, out_shape=jax.ShapeDtypeStruct((OWN, K), F32), in_...  79.2 us

profile of v3, /device:TPU:0, one launch (start us, length us, event | category | flops | bytes accessed | tf_op | source)
XLA Modules:
  0.0 80.8 jit_solution(2118508067535410204)
XLA Ops:
  0.0 79.2 %shard_map.73 = f32[200,256]{1,0:T(8,128)} custom-call(bf16[3072,3200]{1,0:T(8,128)(2,1)} %geno.1, bf16[3200,256]{1,0:T(8,128)(2,1)} %direc.1, bf16[16,200,256]{2,1,0:T(8,128)(2,1)} %bitcast.6, f32[25,128]{1,0:T(8,128)} %bitcast.7, bf16[24,4,128,128]{3,2,1,0:T(8,128)(2,1)} %prec.1, s32[2,16]{1,0:T(2,128)} %bitcast.9, s32[4,24]{1,0:T(4,128)} %bitcast.8, ...), custom_call_target="tpu_custom_call" | custom-call | tf_op jit(solution)/shard_map/pallas_call | solution.py:352
  79.2 1.6 %copy.9 = f32[200,256]{1,0:T(8,128)} copy(f32[200,256]{1,0:T(8,128)} %shard_map.73) | data formatting | bytes 409600

commit v4 on v3

--- a/solution.py
+++ b/solution.py
@@ -24,7 +24,9 @@
 CB = 4
 W = CB * BLK
 NC = NB // CB
+SPLIT = 1664
 NI = 2 * NC
+YFIRST = (6, 11)
 AWAY = ((1, 2), (0, 2), (1, 1), (1, 3), (0, 1), (0, 3), (1, 0))
 F32 = jnp.float32
 BF16 = jnp.bfloat16
@@ -32,9 +34,9 @@
 
 def kernel(
     geno, direc, own_direc, ridge, prec, send_hbm, index_hbm, rel_count, out,
-    g_v, d_v, own_v, ridge_v, ridge_col, prec_v, send_list, rel_index, st, r1p, r1m, r2p, r2m, ry, t_loc, table0, table1, stage, rt, ot, o_full, cx,
+    g_v, d_v, own_v, ridge_v, ridge_col, prec_v, send_list, rel_index, st, r1p, r1m, r2p, r2m, ry, rw, rq, t_loc, table0, table1, stage, rt, ot, o_full, cx,
     d_out, d_in,
-    ld_sem, ldg_sem, a_send, a_recv, b_send, b_recv, c_send, c_recv, x_send, x_recv, d_send, d_recv,
+    ld_sem, ldg_sem, a_send, a_recv, o_send, o_recv, b_send, b_recv, c_send, c_recv, x_send, x_recv, d_send, d_recv,
 ):
     a = lax.axis_index("animal")
     m = lax.axis_index("marker")
@@ -66,7 +68,6 @@
 
     load_d.start()
     load_g(0).start()
-    load_g(1).start()
     barrier = pltpu.get_barrier_semaphore()
 
     def greet(i, carry):
@@ -81,6 +82,7 @@
     load_o.start()
     load_r.start()
     load_d.wait()
+    load_g(1).start()
 
     def krows(i, start, size):
         return pl.ds(pl.multiple_of((i // NC) * HALF + start, KO), size)
@@ -127,18 +129,53 @@
         st[i % NC, own] = st[i % NC, own] + (r2p[i] + r2m[i])
         ay(i).start()
 
+    def settle(h, c, done):
+        done = (done * (1.0 / math.sqrt(MARKERS))).astype(BF16)
+        for b in range(CB):
+            t_loc[h, c * CB + b] = done[:, b * BLK : (b + 1) * BLK]
+            tables[h][c * CB + b] = done[:, b * BLK : (b + 1) * BLK]
+
     def reduce4(i, h):
         ay(i).wait_recv()
-        done = st[i % NC, krows(i, z * 32 + yh * KO, KO)] + ry[i]
-        done = (done * (1.0 / math.sqrt(MARKERS))).astype(BF16)
-        for b in range(CB):
-            t_loc[h, (i % NC) * CB + b] = done[:, b * BLK : (b + 1) * BLK]
-            tables[h][(i % NC) * CB + b] = done[:, b * BLK : (b + 1) * BLK]
-
-    def drain_a(i, carry):
-        for copy in (a1p, a1m, a2p, a2m, ay):
-            copy(i).wait_send()
-        return carry
+        settle(h, i % NC, st[i % NC, krows(i, z * 32 + yh * KO, KO)] + ry[i])
+
+    def o_copy(kind, i):
+        u = YFIRST.index(i)
+        if kind < 4:
+            src, dst, to = krows(i, kind * 32 + (1 - yh) * KO, KO), rw.at[u, kind], across
+        else:
+            to_z = (zo, zp, zm)[kind - 4]
+            src, dst, to = krows(i, to_z * 32 + yh * KO, KO), rq.at[u, kind - 4], to_z * 2 + yh
+        return remote(st.at[i % NC, src], dst, o_send.at[kind, u], o_recv.at[kind, u], marker=to)
+
+    def yfirst1(i):
+        for kind in range(4):
+            o_copy(kind, i).start()
+
+    def yfirst2(i):
+        u = YFIRST.index(i)
+        for kind in range(4):
+            o_copy(kind, i).wait_recv()
+            own = krows(i, kind * 32 + yh * KO, KO)
+            st[i % NC, own] = st[i % NC, own] + rw[u, kind]
+        for kind in range(4, 7):
+            o_copy(kind, i).start()
+
+    def yfirst3(i, h):
+        u = YFIRST.index(i)
+        for kind in range(4, 7):
+            o_copy(kind, i).wait_recv()
+        own = st[i % NC, krows(i, z * 32 + yh * KO, KO)]
+        settle(h, i % NC, own + rq[u, 0] + (rq[u, 1] + rq[u, 2]))
+
+    def drain_a():
+        for i in range(NI):
+            if i in YFIRST:
+                for kind in range(7):
+                    o_copy(kind, i).wait_send()
+            else:
+                for copy in (a1p, a1m, a2p, a2m, ay):
+                    copy(i).wait_send()
 
     def b_copy(h, e, p):
         return remote(
@@ -216,9 +253,6 @@
     def marker_next(h, c):
         ot[...] = ot[...] + marker_part(h, c)
 
-    def marker_last(h):
-        o_full[h] = (ot[...] + marker_part(h, NC - 1)).T
-
     def owner_rows(q, side):
         return pl.ds(pl.multiple_of((2 * q + side) * OWN, 8), OWN)
 
@@ -230,9 +264,13 @@
     def d_copy(h, q, sender):
         return remote(d_out.at[h, q], d_in.at[h, sender], d_send.at[h, q], d_recv.at[h, sender], animal=2 * q + core)
 
-    def cores_out(h):
-        for q in animals_away + [mine]:
-            x_copy(h, q).start()
+    def marker_last(h):
+        rows = slice((NC - 1) * W, NC * W)
+        for lo, hi, side in ((0, SPLIT, 0), (SPLIT, COLS, 1)):
+            part = jnp.dot(rt[NC - 1, h * HALF : (h + 1) * HALF], g_v[rows, lo:hi], preferred_element_type=F32)
+            o_full[h, lo:hi] = (ot[:, lo:hi] + part).T
+            for k in (2, 1, 3, 0):
+                x_copy(h, side * 4 + (x + k) % 4).start()
 
     def chip_sum(h, q):
         x_copy(h, q).wait_recv()
@@ -272,45 +310,47 @@
         lax.fori_loop(0, count, one, 0)
 
     def step_a(it):
-        @pl.when(it < NC)
+        @pl.when(it + 2 < NC)
         def _():
-            @pl.when(it + 2 < NC)
-            def _():
-                load_g(it + 2).start()
-
-            @pl.when(it == NC - 1)
-            def _():
-                load_p.start()
-
-            product(it)
-
-            @pl.when(it == 0)
-            def _():
-                pl.semaphore_wait(barrier, PEERS - 1 + len(AWAY))
+            load_g(it + 2).start()
+
+        @pl.when(it == NC - 2)
+        def _():
+            load_p.start()
+
+        product(it)
+
+        @pl.when(it == 0)
+        def _():
+            pl.semaphore_wait(barrier, PEERS - 1 + len(AWAY))
 
         reduce1(it)
         pl.when(it >= 2)(lambda: reduce2(it - 2))
         pl.when(it >= 4)(lambda: reduce3(it - 4))
-        pl.when(it >= 6)(lambda: reduce4(it - 6, 0))
-
-    each(NI, step_a)
-    load_s.wait()
-    load_i.wait()
-    relatives_out(0)
-    for i in (NI - 2, NI - 1):
-        reduce2(i)
-        reduce3(i - 2)
-        reduce4(i - 4, 1)
-    ridge_column()
-    load_o.wait()
-    for i in (NI - 2, NI - 1):
-        reduce3(i)
-        reduce4(i - 2, 1)
-    load_p.wait()
-    relatives_in(0)
-    relative_sums(0)
-    reduce4(NI - 2, 1)
-    reduce4(NI - 1, 1)
+
+    each(NC, step_a)
+    for it in range(NC, NI + 6):
+        for i, ring, straight in (
+            (it, reduce1, yfirst1),
+            (it - 2, reduce2, yfirst2),
+            (it - 4, reduce3, lambda i: yfirst3(i, i // NC)),
+            (it - 6, lambda i: reduce4(i, i // NC), None),
+        ):
+            if i < NI and i not in YFIRST:
+                ring(i)
+            elif i < NI and straight is not None:
+                straight(i)
+        if it == 2 * NC - 1:
+            load_s.wait()
+            load_i.wait()
+            relatives_out(0)
+        if it == 2 * NC:
+            ridge_column()
+            load_o.wait()
+        if it == 2 * NC + 2:
+            load_p.wait()
+            relatives_in(0)
+            relative_sums(0)
     relatives_out(1)
     relatives_in(1)
     relative_sums(1)
@@ -324,20 +364,17 @@
     each(NC - 2, lambda c: step_m(0, c + 1))
     gather_end(0, NC - 1)
     marker_last(0)
-    cores_out(0)
     gather_end(1, 0)
     marker_first(1)
-    step_m(1, 1)
     owners_out(0)
-    each(NC - 3, lambda c: step_m(1, c + 2))
+    each(NC - 2, lambda c: step_m(1, c + 1))
     gather_end(1, NC - 1)
     marker_last(1)
-    cores_out(1)
+    owners_out(1)
     finish(0)
-    owners_out(1)
     finish(1)
 
-    lax.fori_loop(0, NI, drain_a, 0)
+    drain_a()
     lax.fori_loop(0, NI, drain_c, 0)
     for h in range(2):
         drain_b(h)
@@ -369,6 +406,8 @@
             pltpu.VMEM((NI, 2 * KO, W), F32),
             pltpu.VMEM((NI, 2 * KO, W), F32),
             pltpu.VMEM((NI, KO, W), F32),
+            pltpu.VMEM((len(YFIRST), 4, KO, W), F32),
+            pltpu.VMEM((len(YFIRST), 3, KO, W), F32),
             pltpu.VMEM((2, NB, KO, BLK), BF16),
             pltpu.VMEM((NB + PEERS * SLOTS, KO, BLK), BF16),
             pltpu.VMEM((NB + PEERS * SLOTS, KO, BLK), BF16),
@@ -381,6 +420,7 @@
             pltpu.VMEM((2, 8, OWN, HALF), BF16),
             dma((6,)), dma((NC,)),
             dma((5, NI)), dma((5, NI)),
+            dma((7, len(YFIRST))), dma((7, len(YFIRST))),
             dma((2, PEERS)), dma((2, PEERS)),
             dma((7, NI)), dma((7, NI)),
             dma((2, 8)), dma((2, 8)),

time: 82 us -> 80.4 us (0.980)
  Pallas kernels: 79.2 us -> 77.7 us
    pallas_call x1, Pallas kernels: 79.2 us -> 77.7 us  [local(): pl.pallas_call(kernel, out_shape=jax.ShapeDtypeStruct((OWN, K), F32), in_...]
where the time goes in v4:
time: 80.4 us; the launch traced here: 79.3 us
  Pallas kernels  77.7 us (97%)
  local copies, waits for them, and re-layouts  1.62 us (2%)
    pallas_call x1, Pallas kernels, local(): pl.pallas_call(kernel, out_shape=jax.ShapeDtypeStruct((OWN, K), F32), in_...  77.7 us
    unnamed x1, local copies, waits for them, and re-layouts  1.62 us

profile of v4, /device:TPU:0, one launch (start us, length us, event | category | flops | bytes accessed | tf_op | source)
XLA Modules:
  0.0 79.3 jit_solution(17991282042253925959)
XLA Ops:
  0.0 77.7 %shard_map.73 = f32[200,256]{1,0:T(8,128)} custom-call(bf16[3072,3200]{1,0:T(8,128)(2,1)} %geno.1, bf16[3200,256]{1,0:T(8,128)(2,1)} %direc.1, bf16[16,200,256]{2,1,0:T(8,128)(2,1)} %bitcast.6, f32[25,128]{1,0:T(8,128)} %bitcast.7, bf16[24,4,128,128]{3,2,1,0:T(8,128)(2,1)} %prec.1, s32[2,16]{1,0:T(2,128)} %bitcast.9, s32[4,24]{1,0:T(4,128)} %bitcast.8, ...), custom_call_target="tpu_custom_call" | custom-call | tf_op jit(solution)/shard_map/pallas_call | solution.py:389
  77.7 1.6 %copy.9 = f32[200,256]{1,0:T(8,128)} copy(f32[200,256]{1,0:T(8,128)} %shard_map.73) | data formatting | bytes 409600

commit v5 on v4

--- a/solution.py
+++ b/solution.py
@@ -28,6 +28,8 @@
 NI = 2 * NC
 YFIRST = (6, 11)
 AWAY = ((1, 2), (0, 2), (1, 1), (1, 3), (0, 1), (0, 3), (1, 0))
+ALONG_Y = 6
+RELAYED = ((2, 4), (3, 5), (0, 1))
 F32 = jnp.float32
 BF16 = jnp.bfloat16
 
@@ -206,10 +208,29 @@
 
         lax.fori_loop(1, PEERS, one, 0)
 
-    def c_copy(kind, i, owner):
-        rows = krows(i, owner * KO, KO)
-        to = markers_away[kind][0]
+    def c_copy(kind, i, owner, to):
+        rows = krows(i // NC * NC, owner // 2 * 32 + owner % 2 * KO, KO)
         return remote(rt.at[i % NC, rows], rt.at[i % NC, rows], c_send.at[kind, i], c_recv.at[kind, i], marker=to)
+
+    def c_out(kind, i):
+        return c_copy(kind, i, m, markers_away[kind][0])
+
+    def c_in(kind, i):
+        return c_copy(kind, i, markers_away[kind][1], m)
+
+    def c_relay(kind, i, zfirst):
+        dz = AWAY[kind][1]
+        if zfirst:
+            return c_copy(kind, i, (z + 4 - dz) % 4 * 2 + yh, across)
+        return c_copy(kind, i, across, (z + dz) % 4 * 2 + yh)
+
+    def relay(i, zfirst):
+        if not zfirst:
+            c_in(ALONG_Y, i).wait_recv()
+        for kind, came in RELAYED:
+            if zfirst:
+                c_in(came, i).wait_recv()
+            c_relay(kind, i, zfirst).start()
 
     def relative_sums(h):
         def one(c, carry):
@@ -228,20 +249,40 @@
                     preferred_element_type=F32,
                 )
                 rt[c, krows(i, m * KO, KO), b * BLK : (b + 1) * BLK] = total.astype(BF16)
-            for kind in range(7):
-                c_copy(kind, i, m).start()
+            for kind in (1, 4, 5, 6):
+                c_out(kind, i).start()
+
+            @pl.when(c == NC - 1)
+            def _():
+                for kind, _ in RELAYED:
+                    c_out(kind, i).start()
+
             return carry
 
         lax.fori_loop(0, NC, one, 0)
 
     def drain_c(i, carry):
         for kind in range(7):
-            c_copy(kind, i, m).wait_send()
+            c_out(kind, i).wait_send()
         return carry
 
     def gather_end(h, c):
-        for kind in range(7):
-            c_copy(kind, h * NC + c, markers_away[kind][1]).wait_recv()
+        i = h * NC + c
+
+        @pl.when(c == NC - 1)
+        def _():
+            for kind in range(7):
+                c_in(kind, i).wait_recv()
+
+        @pl.when((c < NC - 1) & (c % 2 == 0))
+        def _():
+            for kind in (0, 2, 3, ALONG_Y):
+                c_in(kind, i).wait_recv()
+
+        @pl.when((c < NC - 1) & (c % 2 == 1))
+        def _():
+            for kind in (0, 1, 2, 3, 4, 5):
+                c_in(kind, i).wait_recv()
 
     def marker_part(h, c):
         rows = pl.ds(pl.multiple_of(c * W, W), W)
@@ -352,6 +393,8 @@
             relatives_in(0)
             relative_sums(0)
     relatives_out(1)
+    for c in range(NC - 1):
+        relay(c, c % 2 == 0)
     relatives_in(1)
     relative_sums(1)
 
@@ -361,7 +404,12 @@
 
     gather_end(0, 0)
     marker_first(0)
-    each(NC - 2, lambda c: step_m(0, c + 1))
+    step_m(0, 1)
+    step_m(0, 2)
+    for c in range(NC - 1):
+        relay(NC + c, c % 2 == 0)
+        if c < NC - 4:
+            step_m(0, c + 3)
     gather_end(0, NC - 1)
     marker_last(0)
     gather_end(1, 0)

time: 80.4 us -> 73.8 us (0.918)
  Pallas kernels: 77.7 us -> 71.1 us
    pallas_call x1, Pallas kernels: 77.7 us -> 71.1 us  [local(): pl.pallas_call(kernel, out_shape=jax.ShapeDtypeStruct((OWN, K), F32), in_...]
where the time goes in v5:
time: 73.8 us; the launch traced here: 72.8 us
  Pallas kernels  71.1 us (96%)
  local copies, waits for them, and re-layouts  1.62 us (2%)
    pallas_call x1, Pallas kernels, local(): pl.pallas_call(kernel, out_shape=jax.ShapeDtypeStruct((OWN, K), F32), in_...  71.1 us
    unnamed x1, local copies, waits for them, and re-layouts  1.62 us

profile of v5, /device:TPU:0, one launch (start us, length us, event | category | flops | bytes accessed | tf_op | source)
XLA Modules:
  0.0 72.8 jit_solution(688586004507440403)
XLA Ops:
  0.0 71.1 %shard_map.73 = f32[200,256]{1,0:T(8,128)} custom-call(bf16[3072,3200]{1,0:T(8,128)(2,1)} %geno.1, bf16[3200,256]{1,0:T(8,128)(2,1)} %direc.1, bf16[16,200,256]{2,1,0:T(8,128)(2,1)} %bitcast.6, f32[25,128]{1,0:T(8,128)} %bitcast.7, bf16[24,4,128,128]{3,2,1,0:T(8,128)(2,1)} %prec.1, s32[2,16]{1,0:T(2,128)} %bitcast.9, s32[4,24]{1,0:T(4,128)} %bitcast.8, ...), custom_call_target="tpu_custom_call" | custom-call | tf_op jit(solution)/shard_map/pallas_call | solution.py:437
  71.1 1.6 %copy.9 = f32[200,256]{1,0:T(8,128)} copy(f32[200,256]{1,0:T(8,128)} %shard_map.73) | data formatting | bytes 409600

commit v6 on v5

--- a/solution.py
+++ b/solution.py
@@ -252,11 +252,6 @@
             for kind in (1, 4, 5, 6):
                 c_out(kind, i).start()
 
-            @pl.when(c == NC - 1)
-            def _():
-                for kind, _ in RELAYED:
-                    c_out(kind, i).start()
-
             return carry
 
         lax.fori_loop(0, NC, one, 0)
@@ -269,17 +264,12 @@
     def gather_end(h, c):
         i = h * NC + c
 
-        @pl.when(c == NC - 1)
-        def _():
-            for kind in range(7):
-                c_in(kind, i).wait_recv()
-
-        @pl.when((c < NC - 1) & (c % 2 == 0))
+        @pl.when(c % 2 == 1)
         def _():
             for kind in (0, 2, 3, ALONG_Y):
                 c_in(kind, i).wait_recv()
 
-        @pl.when((c < NC - 1) & (c % 2 == 1))
+        @pl.when(c % 2 == 0)
         def _():
             for kind in (0, 1, 2, 3, 4, 5):
                 c_in(kind, i).wait_recv()
@@ -393,8 +383,8 @@
             relatives_in(0)
             relative_sums(0)
     relatives_out(1)
-    for c in range(NC - 1):
-        relay(c, c % 2 == 0)
+    for c in range(NC):
+        relay(c, c % 2 == 1)
     relatives_in(1)
     relative_sums(1)
 
@@ -406,8 +396,8 @@
     marker_first(0)
     step_m(0, 1)
     step_m(0, 2)
-    for c in range(NC - 1):
-        relay(NC + c, c % 2 == 0)
+    for c in range(NC):
+        relay(NC + c, c % 2 == 1)
         if c < NC - 4:
             step_m(0, c + 3)
     gather_end(0, NC - 1)

time: 73.8 us -> 72.9 us (0.988); the launches traced: 72.8 us -> 72.7 us
  no operation moved by 1% of the time
where the time goes in v6:
time: 72.9 us; the launch traced here: 72.7 us
  Pallas kernels  71 us (97%)
  local copies, waits for them, and re-layouts  1.62 us (2%)
    pallas_call x1, Pallas kernels, local(): pl.pallas_call(kernel, out_shape=jax.ShapeDtypeStruct((OWN, K), F32), in_...  71 us
    unnamed x1, local copies, waits for them, and re-layouts  1.62 us

profile of v6, /device:TPU:0, one launch (start us, length us, event | category | flops | bytes accessed | tf_op | source)
XLA Modules:
  0.0 72.7 jit_solution(12933899533780593728)
XLA Ops:
  0.0 71.0 %shard_map.73 = f32[200,256]{1,0:T(8,128)} custom-call(bf16[3072,3200]{1,0:T(8,128)(2,1)} %geno.1, bf16[3200,256]{1,0:T(8,128)(2,1)} %direc.1, bf16[16,200,256]{2,1,0:T(8,128)(2,1)} %bitcast.6, f32[25,128]{1,0:T(8,128)} %bitcast.7, bf16[24,4,128,128]{3,2,1,0:T(8,128)(2,1)} %prec.1, s32[2,16]{1,0:T(2,128)} %bitcast.9, s32[4,24]{1,0:T(4,128)} %bitcast.8, ...), custom_call_target="tpu_custom_call" | custom-call | tf_op jit(solution)/shard_map/pallas_call | solution.py:427
  71.0 1.6 %copy.9 = f32[200,256]{1,0:T(8,128)} copy(f32[200,256]{1,0:T(8,128)} %shard_map.73) | data formatting | bytes 409600
